TPU v7x, 128 devices: a whole 4x4x4 slice. The times are simulated.
128 devices in a mesh: group: 8 (over y, x_hi), strip: 16 (over x_lo, z, core).
Axes of the slice: x: 4 (x_hi: 2, x_lo: 2; x = x_hi * 2 + x_lo), y: 4, z: 4, core: 2. Of those that a mesh axis runs over, the one named last changes fastest.
Arguments:
- initial: float32 [8, 512, 1024], P('group', 'strip'), may hold values from -6 to 6
- conductivity: float32 [8, 512, 1024], P('group', 'strip'), may hold values from 0.5 to 1.5
- step_count: int32 [8], P('group'), may hold values from 16 to 32, as said below
- emit_steps: int32 [8, 16], P('group'), may hold values from 1 to 32
- assign: int32 [512], replicated, may hold values from 0 to 127
- sample_inputs: bfloat16 [512, 128], P(('group', 'strip')), may hold values from -6 to 6
- w_first: bfloat16 [128, 512], replicated, may hold values from -0.5 to 0.5
- w_second: bfloat16 [512, 512], replicated, may hold values from -0.25 to 0.25
- w_third: bfloat16 [512, 512], replicated, may hold values from -0.25 to 0.25
- w_out: bfloat16 [512, 512, 1024], P(None, 'strip', 'group'), may hold values from -0.25 to 0.25
Outputs:
- grad_first: float32 [128, 512], replicated
- grad_second: float32 [512, 512], replicated
- grad_third: float32 [512, 512], replicated
- grad_out: bfloat16 [512, 512, 1024], P(None, 'strip', 'group')
Inputs may be any that keep to these rules, and one draw needn't show every extreme that they name: `step_count`: at least 16; some field runs all 32 steps.
All inputs are finite; a program needn't handle non-finite values.
Results may differ from a plain program's by a relative error of at most 0.0039.
The roundings to bfloat16 on the way count: a program that leaves them out, or rounds other values in their place, can miss the bound.
Values may be sent and summed in bfloat16 or wider, within the bound.
A program may use at most 64 MiB of HBM per device.

v0:
```python
import jax
import jax.numpy as jnp
from jax import lax
from jax.sharding import PartitionSpec as P

STEPS = 32
step_rate = 0.125


def padded(x, sides, width):
    for axis, dim in sides:
        count, length = (lax.axis_size(axis), x.shape[dim])
        up = [(i, (i + 1) % count) for i in range(count - 1)]
        down = [(j, i) for i, j in up]
        last = lax.slice_in_dim(x, length - width, length, axis=dim)
        initial = lax.slice_in_dim(x, 0, width, axis=dim)
        before = lax.ppermute(last, axis, up)
        after = lax.ppermute(initial, axis, down)
        x = jnp.concatenate([before, x, after], axis=dim)
    return x


def stencil(current, kappa_rows):
    middle = current[1:-1]
    zero_column = jnp.zeros((middle.shape[0], 1), jnp.float32)
    east_side = jnp.concatenate([middle[:, 1:], zero_column], axis=1)
    west_side = jnp.concatenate([zero_column, middle[:, :-1]], axis=1)
    beside_all = current[2:] + current[:-2] + east_side + west_side
    return middle + step_rate * kappa_rows * (1.0 + 0.25 * jnp.tanh(middle)) * (
        beside_all - 4.0 * middle
    )


def record(history, step_index, inner):
    return lax.dynamic_update_slice_in_dim(history, inner.astype(jnp.bfloat16)[None], step_index, 0)


def contract_rows(left, right):
    return lax.dot_general(
        left, right, (((0,), (0,)), ((), ())), preferred_element_type=jnp.float32
    )


def contract_cols(left, right):
    return lax.dot_general(
        left, right, (((1,), (1,)), ((), ())), preferred_element_type=jnp.float32
    )


def forward(inputs, w_first, w_second, w_third):
    act_a = jnp.tanh(jnp.dot(inputs, w_first, preferred_element_type=jnp.float32))
    hidden_a = act_a.astype(jnp.bfloat16)
    act_b = jnp.tanh(jnp.dot(hidden_a, w_second, preferred_element_type=jnp.float32))
    hidden_b = act_b.astype(jnp.bfloat16)
    act_c = jnp.tanh(jnp.dot(hidden_b, w_third, preferred_element_type=jnp.float32))
    hidden_c = act_c.astype(jnp.bfloat16)
    return ((act_a, act_b, act_c), (hidden_a, hidden_b, hidden_c))


def backward(inputs, activations, hiddens, w_second, w_third, back_c):
    delta_c = (back_c * (1.0 - activations[2] * activations[2])).astype(jnp.bfloat16)
    grad_third = contract_rows(hiddens[1], delta_c)
    back_b = contract_cols(delta_c, w_third)
    delta_b = (back_b * (1.0 - activations[1] * activations[1])).astype(jnp.bfloat16)
    grad_second = contract_rows(hiddens[0], delta_b)
    back_a = contract_cols(delta_b, w_second)
    delta_a = (back_a * (1.0 - activations[0] * activations[0])).astype(jnp.bfloat16)
    grad_first = contract_rows(inputs, delta_a)
    return (grad_first, grad_second, grad_third)


def per_device(
    initial,
    conductivity,
    step_count,
    emit_steps,
    assign,
    sample_inputs,
    w_first,
    w_second,
    w_third,
    w_out,
):
    field_now = initial[0]
    kappa = conductivity[0]
    run_steps = step_count[0]
    emit_row = emit_steps[0]
    row_count = field_now.shape[0]
    start_history = jnp.zeros((STEPS, row_count, field_now.shape[1]), jnp.bfloat16)
    halo_width = 4
    kappa_wide = padded(kappa, (("strip", 0),), halo_width)
    first_row = lax.axis_index("strip") * row_count - halo_width
    global_rows = first_row + jnp.arange(row_count + 2 * halo_width, dtype=jnp.int32)
    inside = ((global_rows >= 0) & (global_rows < row_count * lax.axis_size("strip"))).astype(
        jnp.float32
    )[:, None]

    def block_steps(block_index, carried):
        current, history = carried
        widened = padded(current, (("strip", 0),), halo_width)
        for substep in range(halo_width):
            step_index = block_index * halo_width + substep
            low_row = substep + 1
            span_rows = row_count + 2 * (halo_width - substep - 1)
            candidate = (
                stencil(widened, kappa_wide[low_row : low_row + span_rows])
                * inside[low_row : low_row + span_rows]
            )
            widened = jnp.where(step_index < run_steps, candidate, widened[1:-1])
            offset = halo_width - substep - 1
            history = record(history, step_index, widened[offset : offset + row_count])
        return (widened, history)

    field_now, history = lax.fori_loop(
        0, STEPS // halo_width, block_steps, (field_now, start_history)
    )
    snapshots = jnp.take(history, emit_row - 1, axis=0)
    regrouped = lax.all_to_all(snapshots[None], "group", split_axis=3, concat_axis=0, tiled=True)
    flat_snaps = regrouped.reshape(regrouped.shape[0] * regrouped.shape[1], -1)
    targets = jnp.take(flat_snaps, assign, axis=0)
    weight_flat = w_out.reshape(w_out.shape[0], -1)
    inverse_root = 1.0 / jnp.sqrt(jnp.float32(assign.shape[0]))
    all_inputs = lax.all_gather(sample_inputs, ("group", "strip"), axis=0, tiled=True)
    activations, hiddens = forward(all_inputs, w_first, w_second, w_third)
    hidden_all = hiddens[2]
    predicted = jnp.dot(hidden_all, weight_flat, preferred_element_type=jnp.float32)
    residual = ((predicted - targets.astype(jnp.float32)) * inverse_root).astype(jnp.bfloat16)
    grad_out = contract_rows(hidden_all, residual).astype(jnp.bfloat16)
    residual, grad_out = (residual, grad_out)
    back_c = lax.psum(contract_cols(residual, weight_flat), ("group", "strip"))
    grad_first, grad_second, grad_third = backward(
        all_inputs, activations, hiddens, w_second, w_third, back_c
    )
    return (grad_first, grad_second, grad_third, grad_out.reshape(w_out.shape))


def solution(mesh):
    placed = (
        P("group", "strip", None),
        P("group", "strip", None),
        P("group"),
        P("group", None),
        P(),
        P(("group", "strip"), None),
        P(),
        P(),
        P(),
        P(None, "strip", "group"),
    )
    return jax.shard_map(
        per_device,
        mesh=mesh,
        in_specs=placed,
        out_specs=(P(), P(), P(), P(None, "strip", "group")),
        check_vma=False,
    )
```

profile of v0, /device:TPU:1, one launch (start us, length us, event | category | flops | bytes accessed | tf_op | source)
XLA Modules:
  0.0 374.0 jit_solution(3398122449657235176)
XLA Ops:
  8.9 4.9 %collective-permute-start.2 = (f32[4,1024]{1,0:T(4,128)S(1)}, f32[4,1024]{1,0:T(4,128)S(1)}, u32[]{:S(2)}, u32[]{:S(2)}) collective-permute-start(f32[4,1024]{1,0:T(4,128)S(1)} %get-tuple-element.221), channel_id=1, source_target_pairs={{0,1},{1,2},{2,3},{3,4},{4,5},{5,6},{6,7},{7,8},{8,9},{9,10},{10,1... | collective-permute-start | bytes 49160 | tf_op jit(solution)/shard_map/ppermute | solution.py:17
  20.1 78.7 %while.17 = (s32[]{:T(128)}, f32[32,1024]{1,0:T(8,128)S(1)}, bf16[32,32,1024]{2,1,0:T(8,128)(2,1)S(1)}, s32[]{:T(128)}, f32[40,1024]{1,0:T(8,128)S(1)}, /*index=...) while((s32[]{:T(128)}, f32[32,1024]{1,0:T(8,128)S(1)}, ...), condition=%wide.region_1.2_spmd, body=%wide.region_0.1_spmd.sunk | while | flops 1978390 | bytes 7814625 | solution.py:114
  20.1 2.1 collective-permute-start
  22.2 3.6 collective-permute-start.1
  30.0 2.1 collective-permute-start
  32.0 3.6 collective-permute-start.1
  39.8 2.1 collective-permute-start
  41.9 3.6 collective-permute-start.1
  49.7 2.1 collective-permute-start
  51.7 3.6 collective-permute-start.1
  59.5 2.1 collective-permute-start
  61.6 3.6 collective-permute-start.1
  69.3 2.1 collective-permute-start
  71.4 3.6 collective-permute-start.1
  79.2 2.1 collective-permute-start
  81.2 3.6 collective-permute-start.1
  89.0 2.1 collective-permute-start
  91.1 3.6 collective-permute-start.1
  101.8 4.7 %copy.18 = bf16[1,16,32,1024]{2,1,0,3:T(8,128)(2,1)} copy(bf16[1,16,32,1024]{3,2,1,0:T(8,128)(2,1)S(1)} %bitcast_select_fusion) | data formatting | bytes 2097152 | tf_op jit(solution)/shard_map/jit(_take)/select_n | solution.py:117
  106.5 7.9 %reshape.112 = bf16[8,2,32768]{2,1,0:T(2,128)(2,1)} reshape(bf16[1024,1,16,32]{3,2,1,0:T(8,128)(2,1)} %bitcast.94) | data formatting | bytes 2097152
  114.4 6.7 %all-to-all-start = ((bf16[8,2,32768]{2,1,0:T(2,128)(2,1)}), bf16[8,2,32768]{2,1,0:T(2,128)(2,1)S(1)}, u32[]{:S(2)}, u32[]{:S(2)}) async-start(bf16[8,2,32768]{2,1,0:T(2,128)(2,1)} %reshape.112), calls=%async_computation | async-start | bytes 2097152 | tf_op jit(solution)/shard_map/all_to_all | solution.py:118
  121.1 57.0 %all-gather = bf16[128,4,128]{2,1,0:T(4,128)(2,1)S(1)} all-gather(bf16[1,4,128]{2,1,0:T(4,128)(2,1)S(1)} %bitcast.103), channel_id=1, replica_groups=mesh['group'=8,'strip'=16] {'group','strip'}, dimensions={0}, use_global_device_ids=true | all-gather | bytes 132096 | tf_op jit(solution)/shard_map/all_gather | solution.py:123
  181.3 4.5 %reshape.113 = bf16[1024,1,16,32]{3,2,1,0:T(8,128)(2,1)} reshape(bf16[8,2,32768]{2,1,0:T(2,128)(2,1)S(1)} %all-to-all-done) | data formatting | bytes 2097152
  185.8 5.5 %copy.19 = bf16[1,16,32,8,128]{4,2,1,3,0:T(8,128)(2,1)} copy(bf16[1,16,32,8,128]{2,1,4,3,0:T(8,128)(2,1)} %bitcast.95) | data formatting | bytes 2097152 | tf_op jit(solution)/shard_map/all_to_all | solution.py:118
  193.0 4.4 %gather_fusion.1 = bf16[512,4096]{1,0:T(8,128)(2,1)} fusion(bf16[128,4096]{1,0:T(8,128)(2,1)S(1)} %bitcast.93, s32[1024]{0:T(1024)S(1)} %pad_clamp_fusion), kind=kCustom, calls=%fused_computation.1 | custom fusion | bytes 8390656 | tf_op jit(solution)/shard_map/jit(_take)/gather | solution.py:120
  197.4 6.9 %multiply_convert_fusion = bf16[512,4096]{1,0:T(8,128)(2,1)S(1)} fusion(bf16[512,4096]{1,0:T(8,128)(2,1)} %gather_fusion.1, pred[512]{0:T(512)(128)(4,1)S(1)} %compare_and_fusion.1, bf16[64,8,32,128]{3,2,1,0:T(8,128)(2,1)} %bitcast.104, f32[512,512]{1,0:T(8,128)} %convolution_tanh_fusion), kind=kOutput, calls=%fused_computation.49 | convolution fusion | flops 2158231552 | bytes 13632000 | tf_op jit(solution)/shard_map/dot_general | solution.py:126
  206.3 3.9 %fusion.34 = f32[512,512]{1,0:T(8,128)} fusion(bf16[512,4096]{1,0:T(8,128)(2,1)S(1)} %multiply_convert_fusion, bf16[64,8,32,128]{3,2,1,0:T(8,128)(2,1)S(1)} %bitcast.105), kind=kOutput, calls=%fused_computation.51 | convolution fusion | flops 2147483648 | bytes 9437184 | tf_op jit(solution)/shard_map/dot_general | solution.py:45
  210.2 4.6 %fusion.39 = bf16[64,8,32,128]{3,1,2,0:T(8,128)(2,1)S(1)} fusion(bf16[512,4096]{1,0:T(8,128)(2,1)} %copy-done.5, f32[512,512]{1,0:T(8,128)S(1)} %copy-done.3), kind=kOutput, calls=%fused_computation.56 | convolution fusion | flops 2149842944 | bytes 9437184 | tf_op jit(solution)/shard_map/dot_general | solution.py:39
  214.8 3.3 copy.23
  218.1 139.1 %all-reduce.10.cloned.1.call-done = f32[512,512]{1,0:T(8,128)} async-done(((f32[512,512]{1,0:T(8,128)}), f32[512,512]{1,0:T(8,128)}) %all-reduce.10.cloned.1.call-update) | async-done | bytes 1048592 | tf_op jit(solution)/shard_map/psum | solution.py:130
  360.3 2.1 fusion.43
  362.4 2.5 fusion.52
  (213 shorter events, 34.2 us)
Async XLA Ops:
  7.2 172.8 %copy-start = (bf16[512,512]{1,0:T(8,128)(2,1)S(1)}, bf16[512,512]{1,0:T(8,128)(2,1)}, u32[]{:S(2)}) copy-start(bf16[512,512]{1,0:T(8,128)(2,1)} %param.20) | copy-start | bytes 1572868
  8.9 9.6 %collective-permute-start.2 = (f32[4,1024]{1,0:T(4,128)S(1)}, f32[4,1024]{1,0:T(4,128)S(1)}, u32[]{:S(2)}, u32[]{:S(2)}) collective-permute-start(f32[4,1024]{1,0:T(4,128)S(1)} %get-tuple-element.221), channel_id=1, source_target_pairs={{0,1},{1,2},{2,3},{3,4},{4,5},{5,6},{6,7},{7,8},{8,9},{9,10},{10,1... | collective-permute-start | bytes 49160 | tf_op jit(solution)/shard_map/ppermute | solution.py:17
  13.8 5.1 %collective-permute-start.3 = (f32[4,1024]{1,0:T(4,128)S(1)}, f32[4,1024]{1,0:T(4,128)S(1)}, u32[]{:S(2)}, u32[]{:S(2)}) collective-permute-start(f32[4,1024]{1,0:T(4,128)S(1)} %get-tuple-element.222), channel_id=1, source_target_pairs={{1,0},{2,1},{3,2},{4,3},{5,4},{6,5},{7,6},{8,7},{9,8},{10,9},{11,1... | collective-permute-start | bytes 49160 | tf_op jit(solution)/shard_map/ppermute | solution.py:18
  20.1 9.7 %copy-start.4 = (f32[32,1024]{1,0:T(8,128)S(1)}, f32[32,1024]{1,0:T(8,128)}, u32[]{:S(2)}) copy-start(f32[32,1024]{1,0:T(8,128)} %get-tuple-element.328) | copy-start | bytes 393220 | tf_op jit(solution)/shard_map/while
  20.1 8.6 %collective-permute-start = (f32[4,1024]{1,0:T(4,128)S(1)}, f32[4,1024]{1,0:T(4,128)S(1)}, u32[]{:S(2)}, u32[]{:S(2)}) collective-permute-start(f32[4,1024]{1,0:T(4,128)S(1)} %get-tuple-element.278), channel_id=1, source_target_pairs={{1,0},{2,1},{3,2},{4,3},{5,4},{6,5},{7,6},{8,7},{9,8},{10,9},{11,1... | collective-permute-start | bytes 49160 | tf_op jit(solution)/shard_map/while/body/eval_jaxpr/ppermute | solution.py:18
  22.2 6.6 %collective-permute-start.1 = (f32[4,1024]{1,0:T(4,128)S(1)}, f32[4,1024]{1,0:T(4,128)S(1)}, u32[]{:S(2)}, u32[]{:S(2)}) collective-permute-start(f32[4,1024]{1,0:T(4,128)S(1)} %get-tuple-element.279), channel_id=1, source_target_pairs={{0,1},{1,2},{2,3},{3,4},{4,5},{5,6},{6,7},{7,8},{8,9},{9,10},{10,1... | collective-permute-start | bytes 49160 | tf_op jit(solution)/shard_map/while/body/eval_jaxpr/ppermute | solution.py:17
  29.9 9.7 %copy-start.4 = (f32[32,1024]{1,0:T(8,128)S(1)}, f32[32,1024]{1,0:T(8,128)}, u32[]{:S(2)}) copy-start(f32[32,1024]{1,0:T(8,128)} %get-tuple-element.328) | copy-start | bytes 393220 | tf_op jit(solution)/shard_map/while
  30.0 8.6 %collective-permute-start = (f32[4,1024]{1,0:T(4,128)S(1)}, f32[4,1024]{1,0:T(4,128)S(1)}, u32[]{:S(2)}, u32[]{:S(2)}) collective-permute-start(f32[4,1024]{1,0:T(4,128)S(1)} %get-tuple-element.278), channel_id=1, source_target_pairs={{1,0},{2,1},{3,2},{4,3},{5,4},{6,5},{7,6},{8,7},{9,8},{10,9},{11,1... | collective-permute-start | bytes 49160 | tf_op jit(solution)/shard_map/while/body/eval_jaxpr/ppermute | solution.py:18
  32.0 6.6 %collective-permute-start.1 = (f32[4,1024]{1,0:T(4,128)S(1)}, f32[4,1024]{1,0:T(4,128)S(1)}, u32[]{:S(2)}, u32[]{:S(2)}) collective-permute-start(f32[4,1024]{1,0:T(4,128)S(1)} %get-tuple-element.279), channel_id=1, source_target_pairs={{0,1},{1,2},{2,3},{3,4},{4,5},{5,6},{6,7},{7,8},{8,9},{9,10},{10,1... | collective-permute-start | bytes 49160 | tf_op jit(solution)/shard_map/while/body/eval_jaxpr/ppermute | solution.py:17
  39.8 9.7 %copy-start.4 = (f32[32,1024]{1,0:T(8,128)S(1)}, f32[32,1024]{1,0:T(8,128)}, u32[]{:S(2)}) copy-start(f32[32,1024]{1,0:T(8,128)} %get-tuple-element.328) | copy-start | bytes 393220 | tf_op jit(solution)/shard_map/while
  39.8 8.6 %collective-permute-start = (f32[4,1024]{1,0:T(4,128)S(1)}, f32[4,1024]{1,0:T(4,128)S(1)}, u32[]{:S(2)}, u32[]{:S(2)}) collective-permute-start(f32[4,1024]{1,0:T(4,128)S(1)} %get-tuple-element.278), channel_id=1, source_target_pairs={{1,0},{2,1},{3,2},{4,3},{5,4},{6,5},{7,6},{8,7},{9,8},{10,9},{11,1... | collective-permute-start | bytes 49160 | tf_op jit(solution)/shard_map/while/body/eval_jaxpr/ppermute | solution.py:18
  41.9 6.6 %collective-permute-start.1 = (f32[4,1024]{1,0:T(4,128)S(1)}, f32[4,1024]{1,0:T(4,128)S(1)}, u32[]{:S(2)}, u32[]{:S(2)}) collective-permute-start(f32[4,1024]{1,0:T(4,128)S(1)} %get-tuple-element.279), channel_id=1, source_target_pairs={{0,1},{1,2},{2,3},{3,4},{4,5},{5,6},{6,7},{7,8},{8,9},{9,10},{10,1... | collective-permute-start | bytes 49160 | tf_op jit(solution)/shard_map/while/body/eval_jaxpr/ppermute | solution.py:17
  49.6 9.7 %copy-start.4 = (f32[32,1024]{1,0:T(8,128)S(1)}, f32[32,1024]{1,0:T(8,128)}, u32[]{:S(2)}) copy-start(f32[32,1024]{1,0:T(8,128)} %get-tuple-element.328) | copy-start | bytes 393220 | tf_op jit(solution)/shard_map/while
  49.7 8.6 %collective-permute-start = (f32[4,1024]{1,0:T(4,128)S(1)}, f32[4,1024]{1,0:T(4,128)S(1)}, u32[]{:S(2)}, u32[]{:S(2)}) collective-permute-start(f32[4,1024]{1,0:T(4,128)S(1)} %get-tuple-element.278), channel_id=1, source_target_pairs={{1,0},{2,1},{3,2},{4,3},{5,4},{6,5},{7,6},{8,7},{9,8},{10,9},{11,1... | collective-permute-start | bytes 49160 | tf_op jit(solution)/shard_map/while/body/eval_jaxpr/ppermute | solution.py:18
  51.7 6.6 %collective-permute-start.1 = (f32[4,1024]{1,0:T(4,128)S(1)}, f32[4,1024]{1,0:T(4,128)S(1)}, u32[]{:S(2)}, u32[]{:S(2)}) collective-permute-start(f32[4,1024]{1,0:T(4,128)S(1)} %get-tuple-element.279), channel_id=1, source_target_pairs={{0,1},{1,2},{2,3},{3,4},{4,5},{5,6},{6,7},{7,8},{8,9},{9,10},{10,1... | collective-permute-start | bytes 49160 | tf_op jit(solution)/shard_map/while/body/eval_jaxpr/ppermute | solution.py:17
  59.5 9.7 %copy-start.4 = (f32[32,1024]{1,0:T(8,128)S(1)}, f32[32,1024]{1,0:T(8,128)}, u32[]{:S(2)}) copy-start(f32[32,1024]{1,0:T(8,128)} %get-tuple-element.328) | copy-start | bytes 393220 | tf_op jit(solution)/shard_map/while
  59.5 8.6 %collective-permute-start = (f32[4,1024]{1,0:T(4,128)S(1)}, f32[4,1024]{1,0:T(4,128)S(1)}, u32[]{:S(2)}, u32[]{:S(2)}) collective-permute-start(f32[4,1024]{1,0:T(4,128)S(1)} %get-tuple-element.278), channel_id=1, source_target_pairs={{1,0},{2,1},{3,2},{4,3},{5,4},{6,5},{7,6},{8,7},{9,8},{10,9},{11,1... | collective-permute-start | bytes 49160 | tf_op jit(solution)/shard_map/while/body/eval_jaxpr/ppermute | solution.py:18
  61.6 6.6 %collective-permute-start.1 = (f32[4,1024]{1,0:T(4,128)S(1)}, f32[4,1024]{1,0:T(4,128)S(1)}, u32[]{:S(2)}, u32[]{:S(2)}) collective-permute-start(f32[4,1024]{1,0:T(4,128)S(1)} %get-tuple-element.279), channel_id=1, source_target_pairs={{0,1},{1,2},{2,3},{3,4},{4,5},{5,6},{6,7},{7,8},{8,9},{9,10},{10,1... | collective-permute-start | bytes 49160 | tf_op jit(solution)/shard_map/while/body/eval_jaxpr/ppermute | solution.py:17
  69.3 9.7 %copy-start.4 = (f32[32,1024]{1,0:T(8,128)S(1)}, f32[32,1024]{1,0:T(8,128)}, u32[]{:S(2)}) copy-start(f32[32,1024]{1,0:T(8,128)} %get-tuple-element.328) | copy-start | bytes 393220 | tf_op jit(solution)/shard_map/while
  69.3 8.6 %collective-permute-start = (f32[4,1024]{1,0:T(4,128)S(1)}, f32[4,1024]{1,0:T(4,128)S(1)}, u32[]{:S(2)}, u32[]{:S(2)}) collective-permute-start(f32[4,1024]{1,0:T(4,128)S(1)} %get-tuple-element.278), channel_id=1, source_target_pairs={{1,0},{2,1},{3,2},{4,3},{5,4},{6,5},{7,6},{8,7},{9,8},{10,9},{11,1... | collective-permute-start | bytes 49160 | tf_op jit(solution)/shard_map/while/body/eval_jaxpr/ppermute | solution.py:18
  71.4 6.6 %collective-permute-start.1 = (f32[4,1024]{1,0:T(4,128)S(1)}, f32[4,1024]{1,0:T(4,128)S(1)}, u32[]{:S(2)}, u32[]{:S(2)}) collective-permute-start(f32[4,1024]{1,0:T(4,128)S(1)} %get-tuple-element.279), channel_id=1, source_target_pairs={{0,1},{1,2},{2,3},{3,4},{4,5},{5,6},{6,7},{7,8},{8,9},{9,10},{10,1... | collective-permute-start | bytes 49160 | tf_op jit(solution)/shard_map/while/body/eval_jaxpr/ppermute | solution.py:17
  79.2 9.7 %copy-start.4 = (f32[32,1024]{1,0:T(8,128)S(1)}, f32[32,1024]{1,0:T(8,128)}, u32[]{:S(2)}) copy-start(f32[32,1024]{1,0:T(8,128)} %get-tuple-element.328) | copy-start | bytes 393220 | tf_op jit(solution)/shard_map/while
  79.2 8.6 %collective-permute-start = (f32[4,1024]{1,0:T(4,128)S(1)}, f32[4,1024]{1,0:T(4,128)S(1)}, u32[]{:S(2)}, u32[]{:S(2)}) collective-permute-start(f32[4,1024]{1,0:T(4,128)S(1)} %get-tuple-element.278), channel_id=1, source_target_pairs={{1,0},{2,1},{3,2},{4,3},{5,4},{6,5},{7,6},{8,7},{9,8},{10,9},{11,1... | collective-permute-start | bytes 49160 | tf_op jit(solution)/shard_map/while/body/eval_jaxpr/ppermute | solution.py:18
  81.2 6.6 %collective-permute-start.1 = (f32[4,1024]{1,0:T(4,128)S(1)}, f32[4,1024]{1,0:T(4,128)S(1)}, u32[]{:S(2)}, u32[]{:S(2)}) collective-permute-start(f32[4,1024]{1,0:T(4,128)S(1)} %get-tuple-element.279), channel_id=1, source_target_pairs={{0,1},{1,2},{2,3},{3,4},{4,5},{5,6},{6,7},{7,8},{8,9},{9,10},{10,1... | collective-permute-start | bytes 49160 | tf_op jit(solution)/shard_map/while/body/eval_jaxpr/ppermute | solution.py:17
  89.0 8.6 %collective-permute-start = (f32[4,1024]{1,0:T(4,128)S(1)}, f32[4,1024]{1,0:T(4,128)S(1)}, u32[]{:S(2)}, u32[]{:S(2)}) collective-permute-start(f32[4,1024]{1,0:T(4,128)S(1)} %get-tuple-element.278), channel_id=1, source_target_pairs={{1,0},{2,1},{3,2},{4,3},{5,4},{6,5},{7,6},{8,7},{9,8},{10,9},{11,1... | collective-permute-start | bytes 49160 | tf_op jit(solution)/shard_map/while/body/eval_jaxpr/ppermute | solution.py:18
  91.1 6.6 %collective-permute-start.1 = (f32[4,1024]{1,0:T(4,128)S(1)}, f32[4,1024]{1,0:T(4,128)S(1)}, u32[]{:S(2)}, u32[]{:S(2)}) collective-permute-start(f32[4,1024]{1,0:T(4,128)S(1)} %get-tuple-element.279), channel_id=1, source_target_pairs={{0,1},{1,2},{2,3},{3,4},{4,5},{5,6},{6,7},{7,8},{8,9},{9,10},{10,1... | collective-permute-start | bytes 49160 | tf_op jit(solution)/shard_map/while/body/eval_jaxpr/ppermute | solution.py:17
  106.5 14.6 %copy-start.8 = (bf16[4,128]{1,0:T(4,128)(2,1)S(1)}, bf16[4,128]{1,0:T(4,128)(2,1)}, u32[]{:S(2)}) copy-start(bf16[4,128]{1,0:T(4,128)(2,1)} %param.17) | copy-start | bytes 3076
  106.5 71.7 %copy-start.7 = (bf16[128,512]{1,0:T(8,128)(2,1)S(1)}, bf16[128,512]{1,0:T(8,128)(2,1)}, u32[]{:S(2)}) copy-start(bf16[128,512]{1,0:T(8,128)(2,1)} %param.18) | copy-start | bytes 393220
  106.5 71.9 %copy-start.6 = (bf16[512,512]{1,0:T(8,128)(2,1)S(1)}, bf16[512,512]{1,0:T(8,128)(2,1)}, u32[]{:S(2)}) copy-start(bf16[512,512]{1,0:T(8,128)(2,1)} %param.19) | copy-start | bytes 1572868
  114.4 66.9 %all-to-all-start = ((bf16[8,2,32768]{2,1,0:T(2,128)(2,1)}), bf16[8,2,32768]{2,1,0:T(2,128)(2,1)S(1)}, u32[]{:S(2)}, u32[]{:S(2)}) async-start(bf16[8,2,32768]{2,1,0:T(2,128)(2,1)} %reshape.112), calls=%async_computation | async-start | bytes 2097152 | tf_op jit(solution)/shard_map/all_to_all | solution.py:118
  121.1 236.1 %all-reduce.10.cloned.1.call-start = ((), (), s32[]{:S(2)}) async-start(), calls=%async_computation.1 | async-start | bytes 2097152 | tf_op jit(solution)/shard_map/psum | solution.py:130
  214.8 144.2 %copy-start.2 = (f32[512,512]{1,0:T(8,128)S(1)}, f32[512,512]{1,0:T(8,128)}, u32[]{:S(2)}) copy-start(f32[512,512]{1,0:T(8,128)} %copy-done.1) | copy-start | bytes 3145732
  (5 other events, 25.5 us)
Sparse Core Ops, SparseCore 0:
  210.3 146.8 all-reduce.9
where the time goes:
time: 376 us; the launch traced here: 374 us
  waiting for transfers between devices  140 us (37%)
  starting transfers between devices  59.1 us (16%)
  blocking collectives  57 us (15%)
  local copies, waits for them, and re-layouts  45.6 us (12%)
  matrix products  24.8 us (7%)
  loops' own time  22.1 us (6%)
  between operations  14.2 us (4%)
  other arithmetic  11.6 us (3%)
    psum x1, waiting for transfers between devices, per_device(): back_c = lax.psum(contract_cols(residual, weight_flat), ('group', 'strip'))  139 us
    all_gather x1, blocking collectives, per_device(): lax.all_gather(sample_inputs, ('group', 'strip'), axis=0, tiled=True)  57 us
    ppermute x9, starting transfers between devices, padded(): before = lax.ppermute(last, axis, up)  34 us
    another operation x1, loops' own time, per_device(): lax.fori_loop(0, STEPS // halo_width, block_steps, (field_now, start_hist...  22.1 us
    unnamed x24, local copies, waits for them, and re-layouts  22.1 us
    ppermute x9, starting transfers between devices, padded(): after = lax.ppermute(initial, axis, down)  18.3 us
    dot_general x4, matrix products, contract_rows(): lax.dot_general(left, right, (((0,), (0,)), ((), ())), preferred_element_...  10.6 us
  transfers between devices with their start and end apart: 20, of which 2 were waited for; matrix products, arithmetic and copies ran while one was open for 4% of the time, Pallas kernels for 0%

commit v1 on v0

--- a/solution.py
+++ b/solution.py
@@ -120,7 +120,8 @@
     targets = jnp.take(flat_snaps, assign, axis=0)
     weight_flat = w_out.reshape(w_out.shape[0], -1)
     inverse_root = 1.0 / jnp.sqrt(jnp.float32(assign.shape[0]))
-    all_inputs = lax.all_gather(sample_inputs, ("group", "strip"), axis=0, tiled=True)
+    repeated = jnp.stack([sample_inputs] * lax.axis_size(("group", "strip")))
+    all_inputs = jnp.concatenate(lax.all_to_all(repeated, ("group", "strip"), 0, 0), axis=0)
     activations, hiddens = forward(all_inputs, w_first, w_second, w_third)
     hidden_all = hiddens[2]
     predicted = jnp.dot(hidden_all, weight_flat, preferred_element_type=jnp.float32)

time: 376 us -> 359 us (0.955)
  blocking collectives: 57 us -> 0 us
  waiting for transfers between devices: 140 us -> 168 us
  starting transfers between devices: 59.1 us -> 68.9 us
    all_gather x1 -> x0, blocking collectives: 57 us -> none  [per_device(): lax.all_gather(sample_inputs, ('group', 'strip'), axis=0, tiled=True)]
    psum x1, waiting for transfers between devices: 139 us -> 153 us  [per_device(): back_c = lax.psum(contract_cols(residual, weight_flat), ('group', 'strip'))]
    all_to_all x1, waiting for transfers between devices: 0.01 us -> 13.8 us  [per_device(): lax.all_to_all(snapshots[None], 'group', split_axis=3, concat_axis=0, til...]
    all_to_all x0 -> x1, starting transfers between devices: none -> 11.5 us  [per_device(): lax.all_to_all(repeated, ('group', 'strip'), 0, 0)]
  transfers between devices with their start and end apart: 20 -> 21, of which waited for: 2 -> 3; matrix products, arithmetic and copies ran while one was open for 4% -> 12% of each run, Pallas kernels for 0% -> 0%
where the time goes in v1:
time: 359 us; the launch traced here: 357 us
  waiting for transfers between devices  168 us (47%)
  starting transfers between devices  68.9 us (19%)
  local copies, waits for them, and re-layouts  47 us (13%)
  matrix products  25.5 us (7%)
  loops' own time  22.1 us (6%)
  between operations  14.2 us (4%)
  other arithmetic  11.6 us (3%)
    psum x1, waiting for transfers between devices, per_device(): back_c = lax.psum(contract_cols(residual, weight_flat), ('group', 'strip'))  153 us
    ppermute x9, starting transfers between devices, padded(): before = lax.ppermute(last, axis, up)  32.8 us
    unnamed x24, local copies, waits for them, and re-layouts  22.2 us
    another operation x1, loops' own time, per_device(): lax.fori_loop(0, STEPS // halo_width, block_steps, (field_now, start_hist...  22.1 us
    ppermute x9, starting transfers between devices, padded(): after = lax.ppermute(initial, axis, down)  18.3 us
    all_to_all x1, waiting for transfers between devices, per_device(): lax.all_to_all(snapshots[None], 'group', split_axis=3, concat_axis=0, til...  13.8 us
    all_to_all x1, starting transfers between devices, per_device(): lax.all_to_all(repeated, ('group', 'strip'), 0, 0)  11.5 us
    dot_general x4, matrix products, contract_rows(): lax.dot_general(left, right, (((0,), (0,)), ((), ())), preferred_element_...  11.3 us
  transfers between devices with their start and end apart: 21, of which 3 were waited for; matrix products, arithmetic and copies ran while one was open for 12% of the time, Pallas kernels for 0%

profile of v1, /device:TPU:1, one launch (start us, length us, event | category | flops | bytes accessed | tf_op | source)
XLA Modules:
  0.0 357.0 jit_solution(7118428843459678485)
XLA Ops:
  9.5 11.5 %all-to-all-start = ((bf16[128,4,128]{2,1,0:T(4,128)(2,1)}), bf16[128,4,128]{2,1,0:T(4,128)(2,1)S(1)}, u32[]{:S(2)}, u32[]{:S(2)}) async-start(bf16[128,4,128]{2,1,0:T(4,128)(2,1)} %stack.2), calls=%async_computation | async-start | bytes 262144 | tf_op jit(solution)/shard_map/all_to_all | solution.py:124
  21.8 3.6 %collective-permute-start.2 = (f32[4,1024]{1,0:T(4,128)S(1)}, f32[4,1024]{1,0:T(4,128)S(1)}, u32[]{:S(2)}, u32[]{:S(2)}) collective-permute-start(f32[4,1024]{1,0:T(4,128)S(1)} %get-tuple-element.221), channel_id=1, source_target_pairs={{0,1},{1,2},{2,3},{3,4},{4,5},{5,6},{6,7},{7,8},{8,9},{9,10},{10,1... | collective-permute-start | bytes 49160 | tf_op jit(solution)/shard_map/ppermute | solution.py:17
  32.0 78.7 %while.17 = (s32[]{:T(128)}, f32[32,1024]{1,0:T(8,128)S(1)}, bf16[32,32,1024]{2,1,0:T(8,128)(2,1)S(1)}, s32[]{:T(128)}, f32[40,1024]{1,0:T(8,128)S(1)}, /*index=...) while((s32[]{:T(128)}, f32[32,1024]{1,0:T(8,128)S(1)}, ...), condition=%wide.region_1.2_spmd, body=%wide.region_0.1_spmd.sunk | while | flops 1978390 | bytes 7814625 | solution.py:114
  32.0 2.1 collective-permute-start
  34.1 3.6 %collective-permute-start.1 = (f32[4,1024]{1,0:T(4,128)S(1)}, f32[4,1024]{1,0:T(4,128)S(1)}, u32[]{:S(2)}, u32[]{:S(2)}) collective-permute-start(f32[4,1024]{1,0:T(4,128)S(1)} %get-tuple-element.279), channel_id=1, source_target_pairs={{0,1},{1,2},{2,3},{3,4},{4,5},{5,6},{6,7},{7,8},{8,9},{9,10},{10,1... | collective-permute-start | bytes 49160 | tf_op jit(solution)/shard_map/while/body/eval_jaxpr/ppermute | solution.py:17
  41.9 2.1 collective-permute-start
  43.9 3.6 %collective-permute-start.1 = (f32[4,1024]{1,0:T(4,128)S(1)}, f32[4,1024]{1,0:T(4,128)S(1)}, u32[]{:S(2)}, u32[]{:S(2)}) collective-permute-start(f32[4,1024]{1,0:T(4,128)S(1)} %get-tuple-element.279), channel_id=1, source_target_pairs={{0,1},{1,2},{2,3},{3,4},{4,5},{5,6},{6,7},{7,8},{8,9},{9,10},{10,1... | collective-permute-start | bytes 49160 | tf_op jit(solution)/shard_map/while/body/eval_jaxpr/ppermute | solution.py:17
  51.7 2.1 collective-permute-start
  53.8 3.6 %collective-permute-start.1 = (f32[4,1024]{1,0:T(4,128)S(1)}, f32[4,1024]{1,0:T(4,128)S(1)}, u32[]{:S(2)}, u32[]{:S(2)}) collective-permute-start(f32[4,1024]{1,0:T(4,128)S(1)} %get-tuple-element.279), channel_id=1, source_target_pairs={{0,1},{1,2},{2,3},{3,4},{4,5},{5,6},{6,7},{7,8},{8,9},{9,10},{10,1... | collective-permute-start | bytes 49160 | tf_op jit(solution)/shard_map/while/body/eval_jaxpr/ppermute | solution.py:17
  61.6 2.1 collective-permute-start
  63.6 3.6 %collective-permute-start.1 = (f32[4,1024]{1,0:T(4,128)S(1)}, f32[4,1024]{1,0:T(4,128)S(1)}, u32[]{:S(2)}, u32[]{:S(2)}) collective-permute-start(f32[4,1024]{1,0:T(4,128)S(1)} %get-tuple-element.279), channel_id=1, source_target_pairs={{0,1},{1,2},{2,3},{3,4},{4,5},{5,6},{6,7},{7,8},{8,9},{9,10},{10,1... | collective-permute-start | bytes 49160 | tf_op jit(solution)/shard_map/while/body/eval_jaxpr/ppermute | solution.py:17
  71.4 2.1 collective-permute-start
  73.5 3.6 %collective-permute-start.1 = (f32[4,1024]{1,0:T(4,128)S(1)}, f32[4,1024]{1,0:T(4,128)S(1)}, u32[]{:S(2)}, u32[]{:S(2)}) collective-permute-start(f32[4,1024]{1,0:T(4,128)S(1)} %get-tuple-element.279), channel_id=1, source_target_pairs={{0,1},{1,2},{2,3},{3,4},{4,5},{5,6},{6,7},{7,8},{8,9},{9,10},{10,1... | collective-permute-start | bytes 49160 | tf_op jit(solution)/shard_map/while/body/eval_jaxpr/ppermute | solution.py:17
  81.2 2.1 collective-permute-start
  83.3 3.6 %collective-permute-start.1 = (f32[4,1024]{1,0:T(4,128)S(1)}, f32[4,1024]{1,0:T(4,128)S(1)}, u32[]{:S(2)}, u32[]{:S(2)}) collective-permute-start(f32[4,1024]{1,0:T(4,128)S(1)} %get-tuple-element.279), channel_id=1, source_target_pairs={{0,1},{1,2},{2,3},{3,4},{4,5},{5,6},{6,7},{7,8},{8,9},{9,10},{10,1... | collective-permute-start | bytes 49160 | tf_op jit(solution)/shard_map/while/body/eval_jaxpr/ppermute | solution.py:17
  91.1 2.1 collective-permute-start
  93.1 3.6 %collective-permute-start.1 = (f32[4,1024]{1,0:T(4,128)S(1)}, f32[4,1024]{1,0:T(4,128)S(1)}, u32[]{:S(2)}, u32[]{:S(2)}) collective-permute-start(f32[4,1024]{1,0:T(4,128)S(1)} %get-tuple-element.279), channel_id=1, source_target_pairs={{0,1},{1,2},{2,3},{3,4},{4,5},{5,6},{6,7},{7,8},{8,9},{9,10},{10,1... | collective-permute-start | bytes 49160 | tf_op jit(solution)/shard_map/while/body/eval_jaxpr/ppermute | solution.py:17
  103.0 3.6 %collective-permute-start.1 = (f32[4,1024]{1,0:T(4,128)S(1)}, f32[4,1024]{1,0:T(4,128)S(1)}, u32[]{:S(2)}, u32[]{:S(2)}) collective-permute-start(f32[4,1024]{1,0:T(4,128)S(1)} %get-tuple-element.279), channel_id=1, source_target_pairs={{0,1},{1,2},{2,3},{3,4},{4,5},{5,6},{6,7},{7,8},{8,9},{9,10},{10,1... | collective-permute-start | bytes 49160 | tf_op jit(solution)/shard_map/while/body/eval_jaxpr/ppermute | solution.py:17
  113.7 4.7 %copy.18 = bf16[1,16,32,1024]{2,1,0,3:T(8,128)(2,1)} copy(bf16[1,16,32,1024]{3,2,1,0:T(8,128)(2,1)S(1)} %bitcast_select_fusion) | data formatting | bytes 2097152 | tf_op jit(solution)/shard_map/jit(_take)/select_n | solution.py:117
  118.4 7.9 %reshape.116 = bf16[8,2,32768]{2,1,0:T(2,128)(2,1)} reshape(bf16[1024,1,16,32]{3,2,1,0:T(8,128)(2,1)} %bitcast.93) | data formatting | bytes 2097152
  126.3 6.2 %all-to-all-start.1 = ((bf16[8,2,32768]{2,1,0:T(2,128)(2,1)}), bf16[8,2,32768]{2,1,0:T(2,128)(2,1)S(1)}, u32[]{:S(2)}, u32[]{:S(2)}) async-start(bf16[8,2,32768]{2,1,0:T(2,128)(2,1)} %reshape.116), calls=%async_computation.1 | async-start | bytes 2097152 | tf_op jit(solution)/shard_map/all_to_all | solution.py:118
  135.8 13.8 %all-to-all-done.1 = bf16[8,2,32768]{2,1,0:T(2,128)(2,1)S(1)} async-done(((bf16[8,2,32768]{2,1,0:T(2,128)(2,1)}), bf16[8,2,32768]{2,1,0:T(2,128)(2,1)S(1)}, u32[]{:S(2)}, u32[]{:S(2)}) %all-to-all-start.1) | async-done | bytes 1048608 | tf_op jit(solution)/shard_map/all_to_all | solution.py:118
  149.6 4.5 %reshape.117 = bf16[1024,1,16,32]{3,2,1,0:T(8,128)(2,1)} reshape(bf16[8,2,32768]{2,1,0:T(2,128)(2,1)S(1)} %all-to-all-done.1) | data formatting | bytes 2097152
  154.0 5.5 %copy.19 = bf16[1,16,32,8,128]{4,2,1,3,0:T(8,128)(2,1)} copy(bf16[1,16,32,8,128]{2,1,4,3,0:T(8,128)(2,1)} %bitcast.94) | data formatting | bytes 2097152 | tf_op jit(solution)/shard_map/all_to_all | solution.py:118
  161.3 4.4 %gather_fusion.1 = bf16[512,4096]{1,0:T(8,128)(2,1)} fusion(bf16[128,4096]{1,0:T(8,128)(2,1)S(1)} %bitcast.92, s32[1024]{0:T(1024)S(1)} %pad_clamp_fusion), kind=kCustom, calls=%fused_computation.1 | custom fusion | bytes 8390656 | tf_op jit(solution)/shard_map/jit(_take)/gather | solution.py:120
  165.6 6.9 %multiply_convert_fusion = bf16[512,4096]{1,0:T(8,128)(2,1)S(1)} fusion(bf16[512,4096]{1,0:T(8,128)(2,1)} %gather_fusion.1, pred[512]{0:T(512)(128)(4,1)S(1)} %compare_and_fusion.1, bf16[64,8,32,128]{3,2,1,0:T(8,128)(2,1)} %bitcast.102, f32[512,512]{1,0:T(8,128)} %convolution_tanh_fusion), kind=kOutput, calls=%fused_computation.49 | convolution fusion | flops 2158231552 | bytes 13632000 | tf_op jit(solution)/shard_map/dot_general | solution.py:127
  174.5 3.9 %fusion.34 = f32[512,512]{1,0:T(8,128)} fusion(bf16[512,4096]{1,0:T(8,128)(2,1)S(1)} %multiply_convert_fusion, bf16[64,8,32,128]{3,2,1,0:T(8,128)(2,1)S(1)} %bitcast.103), kind=kOutput, calls=%fused_computation.51 | convolution fusion | flops 2147483648 | bytes 9437184 | tf_op jit(solution)/shard_map/dot_general | solution.py:45
  178.5 4.6 %fusion.39 = bf16[64,8,32,128]{3,1,2,0:T(8,128)(2,1)S(1)} fusion(bf16[512,4096]{1,0:T(8,128)(2,1)} %copy-done.5, f32[512,512]{1,0:T(8,128)S(1)} %copy-done.3), kind=kOutput, calls=%fused_computation.56 | convolution fusion | flops 2149842944 | bytes 9437184 | tf_op jit(solution)/shard_map/dot_general | solution.py:39
  183.1 3.3 copy.23
  186.3 153.1 %all-reduce.10.cloned.1.call-done = f32[512,512]{1,0:T(8,128)} async-done(((f32[512,512]{1,0:T(8,128)}), f32[512,512]{1,0:T(8,128)}) %all-reduce.10.cloned.1.call-update) | async-done | bytes 1048592 | tf_op jit(solution)/shard_map/psum | solution.py:131
  342.6 2.8 fusion.43
  345.4 2.5 fusion.52
  (215 shorter events, 37.9 us)
Async XLA Ops:
  7.2 127.2 %copy-start = (bf16[512,512]{1,0:T(8,128)(2,1)S(1)}, bf16[512,512]{1,0:T(8,128)(2,1)}, u32[]{:S(2)}) copy-start(bf16[512,512]{1,0:T(8,128)(2,1)} %param.20) | copy-start | bytes 1572868
  9.5 116.8 %all-to-all-start = ((bf16[128,4,128]{2,1,0:T(4,128)(2,1)}), bf16[128,4,128]{2,1,0:T(4,128)(2,1)S(1)}, u32[]{:S(2)}, u32[]{:S(2)}) async-start(bf16[128,4,128]{2,1,0:T(4,128)(2,1)} %stack.2), calls=%async_computation | async-start | bytes 262144 | tf_op jit(solution)/shard_map/all_to_all | solution.py:124
  21.8 8.3 %collective-permute-start.2 = (f32[4,1024]{1,0:T(4,128)S(1)}, f32[4,1024]{1,0:T(4,128)S(1)}, u32[]{:S(2)}, u32[]{:S(2)}) collective-permute-start(f32[4,1024]{1,0:T(4,128)S(1)} %get-tuple-element.221), channel_id=1, source_target_pairs={{0,1},{1,2},{2,3},{3,4},{4,5},{5,6},{6,7},{7,8},{8,9},{9,10},{10,1... | collective-permute-start | bytes 49160 | tf_op jit(solution)/shard_map/ppermute | solution.py:17
  25.4 5.4 %collective-permute-start.3 = (f32[4,1024]{1,0:T(4,128)S(1)}, f32[4,1024]{1,0:T(4,128)S(1)}, u32[]{:S(2)}, u32[]{:S(2)}) collective-permute-start(f32[4,1024]{1,0:T(4,128)S(1)} %get-tuple-element.222), channel_id=1, source_target_pairs={{1,0},{2,1},{3,2},{4,3},{5,4},{6,5},{7,6},{8,7},{9,8},{10,9},{11,1... | collective-permute-start | bytes 49160 | tf_op jit(solution)/shard_map/ppermute | solution.py:18
  32.0 9.7 %copy-start.4 = (f32[32,1024]{1,0:T(8,128)S(1)}, f32[32,1024]{1,0:T(8,128)}, u32[]{:S(2)}) copy-start(f32[32,1024]{1,0:T(8,128)} %get-tuple-element.328) | copy-start | bytes 393220 | tf_op jit(solution)/shard_map/while
  32.0 8.6 %collective-permute-start = (f32[4,1024]{1,0:T(4,128)S(1)}, f32[4,1024]{1,0:T(4,128)S(1)}, u32[]{:S(2)}, u32[]{:S(2)}) collective-permute-start(f32[4,1024]{1,0:T(4,128)S(1)} %get-tuple-element.278), channel_id=1, source_target_pairs={{1,0},{2,1},{3,2},{4,3},{5,4},{6,5},{7,6},{8,7},{9,8},{10,9},{11,1... | collective-permute-start | bytes 49160 | tf_op jit(solution)/shard_map/while/body/eval_jaxpr/ppermute | solution.py:18
  34.1 6.6 %collective-permute-start.1 = (f32[4,1024]{1,0:T(4,128)S(1)}, f32[4,1024]{1,0:T(4,128)S(1)}, u32[]{:S(2)}, u32[]{:S(2)}) collective-permute-start(f32[4,1024]{1,0:T(4,128)S(1)} %get-tuple-element.279), channel_id=1, source_target_pairs={{0,1},{1,2},{2,3},{3,4},{4,5},{5,6},{6,7},{7,8},{8,9},{9,10},{10,1... | collective-permute-start | bytes 49160 | tf_op jit(solution)/shard_map/while/body/eval_jaxpr/ppermute | solution.py:17
  41.8 9.7 %copy-start.4 = (f32[32,1024]{1,0:T(8,128)S(1)}, f32[32,1024]{1,0:T(8,128)}, u32[]{:S(2)}) copy-start(f32[32,1024]{1,0:T(8,128)} %get-tuple-element.328) | copy-start | bytes 393220 | tf_op jit(solution)/shard_map/while
  41.9 8.6 %collective-permute-start = (f32[4,1024]{1,0:T(4,128)S(1)}, f32[4,1024]{1,0:T(4,128)S(1)}, u32[]{:S(2)}, u32[]{:S(2)}) collective-permute-start(f32[4,1024]{1,0:T(4,128)S(1)} %get-tuple-element.278), channel_id=1, source_target_pairs={{1,0},{2,1},{3,2},{4,3},{5,4},{6,5},{7,6},{8,7},{9,8},{10,9},{11,1... | collective-permute-start | bytes 49160 | tf_op jit(solution)/shard_map/while/body/eval_jaxpr/ppermute | solution.py:18
  43.9 6.6 %collective-permute-start.1 = (f32[4,1024]{1,0:T(4,128)S(1)}, f32[4,1024]{1,0:T(4,128)S(1)}, u32[]{:S(2)}, u32[]{:S(2)}) collective-permute-start(f32[4,1024]{1,0:T(4,128)S(1)} %get-tuple-element.279), channel_id=1, source_target_pairs={{0,1},{1,2},{2,3},{3,4},{4,5},{5,6},{6,7},{7,8},{8,9},{9,10},{10,1... | collective-permute-start | bytes 49160 | tf_op jit(solution)/shard_map/while/body/eval_jaxpr/ppermute | solution.py:17
  51.7 9.7 %copy-start.4 = (f32[32,1024]{1,0:T(8,128)S(1)}, f32[32,1024]{1,0:T(8,128)}, u32[]{:S(2)}) copy-start(f32[32,1024]{1,0:T(8,128)} %get-tuple-element.328) | copy-start | bytes 393220 | tf_op jit(solution)/shard_map/while
  51.7 8.6 %collective-permute-start = (f32[4,1024]{1,0:T(4,128)S(1)}, f32[4,1024]{1,0:T(4,128)S(1)}, u32[]{:S(2)}, u32[]{:S(2)}) collective-permute-start(f32[4,1024]{1,0:T(4,128)S(1)} %get-tuple-element.278), channel_id=1, source_target_pairs={{1,0},{2,1},{3,2},{4,3},{5,4},{6,5},{7,6},{8,7},{9,8},{10,9},{11,1... | collective-permute-start | bytes 49160 | tf_op jit(solution)/shard_map/while/body/eval_jaxpr/ppermute | solution.py:18
  53.8 6.6 %collective-permute-start.1 = (f32[4,1024]{1,0:T(4,128)S(1)}, f32[4,1024]{1,0:T(4,128)S(1)}, u32[]{:S(2)}, u32[]{:S(2)}) collective-permute-start(f32[4,1024]{1,0:T(4,128)S(1)} %get-tuple-element.279), channel_id=1, source_target_pairs={{0,1},{1,2},{2,3},{3,4},{4,5},{5,6},{6,7},{7,8},{8,9},{9,10},{10,1... | collective-permute-start | bytes 49160 | tf_op jit(solution)/shard_map/while/body/eval_jaxpr/ppermute | solution.py:17
  61.5 9.7 %copy-start.4 = (f32[32,1024]{1,0:T(8,128)S(1)}, f32[32,1024]{1,0:T(8,128)}, u32[]{:S(2)}) copy-start(f32[32,1024]{1,0:T(8,128)} %get-tuple-element.328) | copy-start | bytes 393220 | tf_op jit(solution)/shard_map/while
  61.6 8.6 %collective-permute-start = (f32[4,1024]{1,0:T(4,128)S(1)}, f32[4,1024]{1,0:T(4,128)S(1)}, u32[]{:S(2)}, u32[]{:S(2)}) collective-permute-start(f32[4,1024]{1,0:T(4,128)S(1)} %get-tuple-element.278), channel_id=1, source_target_pairs={{1,0},{2,1},{3,2},{4,3},{5,4},{6,5},{7,6},{8,7},{9,8},{10,9},{11,1... | collective-permute-start | bytes 49160 | tf_op jit(solution)/shard_map/while/body/eval_jaxpr/ppermute | solution.py:18
  63.6 6.6 %collective-permute-start.1 = (f32[4,1024]{1,0:T(4,128)S(1)}, f32[4,1024]{1,0:T(4,128)S(1)}, u32[]{:S(2)}, u32[]{:S(2)}) collective-permute-start(f32[4,1024]{1,0:T(4,128)S(1)} %get-tuple-element.279), channel_id=1, source_target_pairs={{0,1},{1,2},{2,3},{3,4},{4,5},{5,6},{6,7},{7,8},{8,9},{9,10},{10,1... | collective-permute-start | bytes 49160 | tf_op jit(solution)/shard_map/while/body/eval_jaxpr/ppermute | solution.py:17
  71.4 9.7 %copy-start.4 = (f32[32,1024]{1,0:T(8,128)S(1)}, f32[32,1024]{1,0:T(8,128)}, u32[]{:S(2)}) copy-start(f32[32,1024]{1,0:T(8,128)} %get-tuple-element.328) | copy-start | bytes 393220 | tf_op jit(solution)/shard_map/while
  71.4 8.6 %collective-permute-start = (f32[4,1024]{1,0:T(4,128)S(1)}, f32[4,1024]{1,0:T(4,128)S(1)}, u32[]{:S(2)}, u32[]{:S(2)}) collective-permute-start(f32[4,1024]{1,0:T(4,128)S(1)} %get-tuple-element.278), channel_id=1, source_target_pairs={{1,0},{2,1},{3,2},{4,3},{5,4},{6,5},{7,6},{8,7},{9,8},{10,9},{11,1... | collective-permute-start | bytes 49160 | tf_op jit(solution)/shard_map/while/body/eval_jaxpr/ppermute | solution.py:18
  73.5 6.6 %collective-permute-start.1 = (f32[4,1024]{1,0:T(4,128)S(1)}, f32[4,1024]{1,0:T(4,128)S(1)}, u32[]{:S(2)}, u32[]{:S(2)}) collective-permute-start(f32[4,1024]{1,0:T(4,128)S(1)} %get-tuple-element.279), channel_id=1, source_target_pairs={{0,1},{1,2},{2,3},{3,4},{4,5},{5,6},{6,7},{7,8},{8,9},{9,10},{10,1... | collective-permute-start | bytes 49160 | tf_op jit(solution)/shard_map/while/body/eval_jaxpr/ppermute | solution.py:17
  81.2 9.7 %copy-start.4 = (f32[32,1024]{1,0:T(8,128)S(1)}, f32[32,1024]{1,0:T(8,128)}, u32[]{:S(2)}) copy-start(f32[32,1024]{1,0:T(8,128)} %get-tuple-element.328) | copy-start | bytes 393220 | tf_op jit(solution)/shard_map/while
  81.2 8.6 %collective-permute-start = (f32[4,1024]{1,0:T(4,128)S(1)}, f32[4,1024]{1,0:T(4,128)S(1)}, u32[]{:S(2)}, u32[]{:S(2)}) collective-permute-start(f32[4,1024]{1,0:T(4,128)S(1)} %get-tuple-element.278), channel_id=1, source_target_pairs={{1,0},{2,1},{3,2},{4,3},{5,4},{6,5},{7,6},{8,7},{9,8},{10,9},{11,1... | collective-permute-start | bytes 49160 | tf_op jit(solution)/shard_map/while/body/eval_jaxpr/ppermute | solution.py:18
  83.3 6.6 %collective-permute-start.1 = (f32[4,1024]{1,0:T(4,128)S(1)}, f32[4,1024]{1,0:T(4,128)S(1)}, u32[]{:S(2)}, u32[]{:S(2)}) collective-permute-start(f32[4,1024]{1,0:T(4,128)S(1)} %get-tuple-element.279), channel_id=1, source_target_pairs={{0,1},{1,2},{2,3},{3,4},{4,5},{5,6},{6,7},{7,8},{8,9},{9,10},{10,1... | collective-permute-start | bytes 49160 | tf_op jit(solution)/shard_map/while/body/eval_jaxpr/ppermute | solution.py:17
  91.0 9.7 %copy-start.4 = (f32[32,1024]{1,0:T(8,128)S(1)}, f32[32,1024]{1,0:T(8,128)}, u32[]{:S(2)}) copy-start(f32[32,1024]{1,0:T(8,128)} %get-tuple-element.328) | copy-start | bytes 393220 | tf_op jit(solution)/shard_map/while
  91.1 8.6 %collective-permute-start = (f32[4,1024]{1,0:T(4,128)S(1)}, f32[4,1024]{1,0:T(4,128)S(1)}, u32[]{:S(2)}, u32[]{:S(2)}) collective-permute-start(f32[4,1024]{1,0:T(4,128)S(1)} %get-tuple-element.278), channel_id=1, source_target_pairs={{1,0},{2,1},{3,2},{4,3},{5,4},{6,5},{7,6},{8,7},{9,8},{10,9},{11,1... | collective-permute-start | bytes 49160 | tf_op jit(solution)/shard_map/while/body/eval_jaxpr/ppermute | solution.py:18
  93.1 6.6 %collective-permute-start.1 = (f32[4,1024]{1,0:T(4,128)S(1)}, f32[4,1024]{1,0:T(4,128)S(1)}, u32[]{:S(2)}, u32[]{:S(2)}) collective-permute-start(f32[4,1024]{1,0:T(4,128)S(1)} %get-tuple-element.279), channel_id=1, source_target_pairs={{0,1},{1,2},{2,3},{3,4},{4,5},{5,6},{6,7},{7,8},{8,9},{9,10},{10,1... | collective-permute-start | bytes 49160 | tf_op jit(solution)/shard_map/while/body/eval_jaxpr/ppermute | solution.py:17
  100.9 8.6 %collective-permute-start = (f32[4,1024]{1,0:T(4,128)S(1)}, f32[4,1024]{1,0:T(4,128)S(1)}, u32[]{:S(2)}, u32[]{:S(2)}) collective-permute-start(f32[4,1024]{1,0:T(4,128)S(1)} %get-tuple-element.278), channel_id=1, source_target_pairs={{1,0},{2,1},{3,2},{4,3},{5,4},{6,5},{7,6},{8,7},{9,8},{10,9},{11,1... | collective-permute-start | bytes 49160 | tf_op jit(solution)/shard_map/while/body/eval_jaxpr/ppermute | solution.py:18
  103.0 6.6 %collective-permute-start.1 = (f32[4,1024]{1,0:T(4,128)S(1)}, f32[4,1024]{1,0:T(4,128)S(1)}, u32[]{:S(2)}, u32[]{:S(2)}) collective-permute-start(f32[4,1024]{1,0:T(4,128)S(1)} %get-tuple-element.279), channel_id=1, source_target_pairs={{0,1},{1,2},{2,3},{3,4},{4,5},{5,6},{6,7},{7,8},{8,9},{9,10},{10,1... | collective-permute-start | bytes 49160 | tf_op jit(solution)/shard_map/while/body/eval_jaxpr/ppermute | solution.py:17
  118.4 14.2 %copy-start.8 = (bf16[128,512]{1,0:T(8,128)(2,1)S(1)}, bf16[128,512]{1,0:T(8,128)(2,1)}, u32[]{:S(2)}) copy-start(bf16[128,512]{1,0:T(8,128)(2,1)} %param.18) | copy-start | bytes 393220
  118.4 14.5 %copy-start.6 = (bf16[512,512]{1,0:T(8,128)(2,1)S(1)}, bf16[512,512]{1,0:T(8,128)(2,1)}, u32[]{:S(2)}) copy-start(bf16[512,512]{1,0:T(8,128)(2,1)} %param.19) | copy-start | bytes 1572868
  126.3 23.3 %all-to-all-start.1 = ((bf16[8,2,32768]{2,1,0:T(2,128)(2,1)}), bf16[8,2,32768]{2,1,0:T(2,128)(2,1)S(1)}, u32[]{:S(2)}, u32[]{:S(2)}) async-start(bf16[8,2,32768]{2,1,0:T(2,128)(2,1)} %reshape.116), calls=%async_computation.1 | async-start | bytes 2097152 | tf_op jit(solution)/shard_map/all_to_all | solution.py:118
  132.6 206.9 %all-reduce.10.cloned.1.call-start = ((), (), s32[]{:S(2)}) async-start(), calls=%async_computation.2 | async-start | bytes 2097152 | tf_op jit(solution)/shard_map/psum | solution.py:131
  183.1 158.2 %copy-start.2 = (f32[512,512]{1,0:T(8,128)S(1)}, f32[512,512]{1,0:T(8,128)}, u32[]{:S(2)}) copy-start(f32[512,512]{1,0:T(8,128)} %copy-done.1) | copy-start | bytes 3145732
  (6 other events, 29.5 us)
Sparse Core Ops, SparseCore 0:
  178.6 160.8 all-reduce.9
